TPU v7x, 32 devices: a whole 2x2x4 slice. The times are simulated.
32 devices in a mesh: group: 2 (over x), expert: 16 (over z, y, core).
Axes of the slice: x: 2, y: 2, z: 4, core: 2. Of those that a mesh axis runs over, the one named last changes fastest.
Arguments:
- tokens: bfloat16 [64, 256, 1024], P(('group', 'expert')), parts along dimension 0, may hold values from -6 to 6
- w_qkv: bfloat16 [1024, 3072], P('expert'), may hold values from -0.1875 to 0.1875
- w_attn_out: bfloat16 [1024, 1024], P('expert'), may hold values from -0.1875 to 0.1875
- slot_keys: bfloat16 [1024, 32], replicated, may hold values from -0.5 to 0.5
- w_expert_in: bfloat16 [16, 1024, 2048], P('expert'), may hold values from -0.375 to 0.375
- w_expert_out: bfloat16 [16, 2048, 1024], P('expert'), may hold values from -0.125 to 0.125
Outputs:
- block_out: bfloat16 [64, 256, 1024], P(('group', 'expert')), parts along dimension 0
There are 2 independent parts, one for each index of `group`. A program takes and returns all parts, laid end to end along the dimension named above; an argument that names none is the same for every part. Nothing has to cross between parts.
All inputs are finite; a program needn't handle non-finite values.
Results may differ from a plain program's by a relative error of at most 0.009.
Values may be sent and summed in bfloat16 or wider, within the bound.
No kernel may reach another device: no remote copies, remote signals or barrier semaphores. Data moves between devices by JAX's collectives and lax.ppermute only.
A program may use at most 64 MiB of HBM per device.

v0:
```python
import math
import jax
import jax.numpy as jnp
from jax import lax
from jax.sharding import PartitionSpec as P

HEADS = 16


def layer_norm(values):
    center = values - jnp.mean(values, axis=-1, keepdims=True)
    spread = jnp.mean(center * center, axis=-1, keepdims=True)
    return center * lax.rsqrt(spread + 1e-06)


def on_device(tokens, w_qkv, w_attn_out, slot_keys, w_expert_in, w_expert_out):
    image_count, length, model_width = tokens.shape
    head_count = HEADS
    head_width = model_width // head_count
    row_count = image_count * length
    normed = (
        layer_norm(tokens.astype(jnp.float32)).astype(jnp.bfloat16).reshape(row_count, model_width)
    )
    full_qkv = lax.all_gather(w_qkv, "expert", axis=0, tiled=True)
    qkv = jnp.dot(normed, full_qkv, preferred_element_type=jnp.float32)
    packed = qkv.astype(jnp.bfloat16).reshape(image_count, length, 3, head_count, head_width)
    query = packed[:, :, 0]
    keys = packed[:, :, 1]
    values = packed[:, :, 2]
    scores = jnp.einsum(
        "bqhd,bkhd->bhqk", query, keys, preferred_element_type=jnp.float32
    ) / math.sqrt(head_width)
    weights = jax.nn.softmax(scores, axis=-1).astype(jnp.bfloat16)
    attended = jnp.einsum(
        "bhqk,bkhd->bqhd", weights, values, preferred_element_type=jnp.float32
    ).astype(jnp.bfloat16)
    attended = attended.reshape(row_count, model_width)
    full_out = lax.all_gather(w_attn_out, "expert", axis=0, tiled=True)
    projected = jnp.dot(attended, full_out, preferred_element_type=jnp.float32)
    resid = tokens.astype(jnp.float32) + projected.reshape(image_count, length, model_width)
    normed_two = layer_norm(resid).astype(jnp.bfloat16)
    slot_count = slot_keys.shape[1]
    logits = jnp.dot(
        normed_two.reshape(row_count, model_width), slot_keys, preferred_element_type=jnp.float32
    )
    logits = logits.reshape(image_count, length, slot_count)
    dispatch = jax.nn.softmax(logits, axis=1).astype(jnp.bfloat16)
    combine = jax.nn.softmax(logits, axis=2).astype(jnp.bfloat16)
    slot_inputs = jnp.einsum(
        "bsn,bsd->bnd", dispatch, normed_two, preferred_element_type=jnp.float32
    ).astype(jnp.bfloat16)
    sources = lax.axis_size("expert")
    expert_here = w_expert_in.shape[0]
    pairs = slot_count // (sources * expert_here)
    block = lax.all_to_all(slot_inputs, "expert", split_axis=1, concat_axis=1, tiled=True)
    batch = block.shape[0]
    arranged = block.reshape(batch, sources, expert_here, pairs, model_width)
    hidden = jnp.einsum(
        "bnepd,edh->bneph", arranged, w_expert_in, preferred_element_type=jnp.float32
    )
    hidden = jax.nn.gelu(hidden, approximate=False).astype(jnp.bfloat16)
    answer = jnp.einsum(
        "bneph,ehd->bnepd", hidden, w_expert_out, preferred_element_type=jnp.float32
    )
    answered = answer.astype(jnp.bfloat16).reshape(batch, slot_count, model_width)
    slot_outputs = lax.all_to_all(answered, "expert", split_axis=1, concat_axis=1, tiled=True)
    mixed = jnp.einsum("bsn,bnd->bsd", combine, slot_outputs, preferred_element_type=jnp.float32)
    return (resid + mixed).astype(jnp.bfloat16)


def solution(mesh):
    placed = (
        P(("group", "expert"), None, None),
        P("expert", None),
        P("expert", None),
        P(),
        P("expert", None, None),
        P("expert", None, None),
    )
    return jax.shard_map(
        on_device,
        mesh=mesh,
        in_specs=placed,
        out_specs=P(("group", "expert"), None, None),
        check_vma=False,
    )
```

profile of v0, /device:TPU:0, one launch (start us, length us, event | category | flops | bytes accessed | tf_op | source)
XLA Modules:
  0.0 159.9 jit_solution(4813306679087702941)
XLA Ops:
  6.5 0.0 copy-start
  6.5 0.0 copy-start.1
  6.5 0.0 all-gather.3.cloned.1.call-start
  6.5 0.7 all-gather.3.cloned.1.call-update
  7.3 0.0 all-gather.5.cloned.1.call-start
  7.3 0.7 all-gather.5.cloned.1.call-update
  8.0 1.4 convert_reduce_fusion
  9.5 0.0 copy-done.1
  9.5 0.4 fusion.14
  9.9 0.3 fusion.15
  10.2 64.0 %all-gather.3.cloned.1.call-done = bf16[1024,3072]{1,0:T(8,128)(2,1)} async-done(((bf16[64,3072]{1,0:T(8,128)(2,1)}), bf16[1024,3072]{1,0:T(8,128)(2,1)}) %all-gather.3.cloned.1.call-update) | async-done | bytes 6291472 | tf_op jit(solution)/shard_map/all_gather | solution.py:24
  74.2 7.5 %convolution_convert_fusion = bf16[512,3072]{1,0:T(8,128)(2,1)} fusion(bf16[512,1024]{1,0:T(8,128)(2,1)S(1)} %bitcast.133, bf16[1024,3072]{1,0:T(8,128)(2,1)} %all-gather.3.cloned.1.call-done), kind=kOutput, calls=%fused_computation.7 | convolution fusion | flops 3222798336 | bytes 10485760 | tf_op jit(solution)/shard_map/dot_general | solution.py:25
  81.8 8.6 %reshape.80 = bf16[2,256,3,16,64]{4,3,2,1,0:T(8,128)(2,1)} reshape(bf16[512,3072]{1,0:T(8,128)(2,1)} %convolution_convert_fusion) | data formatting | bytes 6291456 | tf_op jit(solution)/shard_map/reshape | solution.py:26
  90.4 6.0 %fusion.110 = (bf16[2,256,1,16,64]{4,3,2,1,0:T(8,128)(2,1)S(1)}, bf16[2,256,1,16,64]{4,3,2,1,0:T(8,128)(2,1)}, bf16[2,256,1,16,64]{4,3,2,1,0:T(8,128)(2,1)}) fusion(bf16[2,256,3,16,64]{4,3,2,1,0:T(8,128)(2,1)} %reshape.80), kind=kLoop, calls=%fused_computation.118 | loop fusion | bytes 6291456 | tf_op jit(solution)/shard_map/slice | solution.py:29
  96.4 3.6 %copy.48 = bf16[2,256,1,16,64]{1,4,3,0,2:T(8,128)(2,1)} copy(bf16[2,256,1,16,64]{4,3,2,1,0:T(8,128)(2,1)} %get-tuple-element.6) | data formatting | bytes 2097152
  99.9 3.5 %copy.49 = bf16[2,256,1,16,64]{1,4,3,0,2:T(8,128)(2,1)} copy(bf16[2,256,1,16,64]{4,3,2,1,0:T(8,128)(2,1)} %get-tuple-element.7) | data formatting | bytes 2097152
  103.5 2.5 %copy.47 = bf16[2,256,1,16,64]{1,4,3,0,2:T(8,128)(2,1)} copy(bf16[2,256,1,16,64]{4,3,2,1,0:T(8,128)(2,1)S(1)} %get-tuple-element.5) | data formatting | bytes 2097152
  106.0 2.8 %fusion.31 = f32[2,16,256,256]{2,3,1,0:T(8,128)S(1)} fusion(bf16[2,256,1,16,64]{1,4,3,0,2:T(8,128)(2,1)} %copy.49, bf16[2,256,1,16,64]{1,4,3,0,2:T(8,128)(2,1)} %copy.48), kind=kOutput, calls=%fused_computation.34 | convolution fusion | flops 268435456 | bytes 10485760 | tf_op jit(solution)/shard_map/bqhd,bkhd->bhqk/dot_general | solution.py:30
  108.8 0.0 copy-start.2
  108.8 6.3 %fusion.111 = (f32[2,16,256]{2,1,0:T(8,128)S(1)}, f32[2,16,256,256]{2,3,1,0:T(8,128)S(1)}) fusion(f32[2,16,256,256]{2,3,1,0:T(8,128)S(1)} %fusion.31), kind=kOutput, calls=%fused_computation.119 | output fusion | flops 8388863 | bytes 16809984 | tf_op jit(solution)/shard_map/sub | solution.py:33
  115.1 0.0 copy-done.2
  115.1 1.8 %fusion.20 = bf16[2,16,64,256]{3,2,1,0:T(8,128)(2,1)} fusion(f32[2,16,256,256]{2,3,1,0:T(8,128)S(1)} %get-tuple-element.9, f32[2,16,256]{2,1,0:T(8,128)S(1)} %get-tuple-element.8, bf16[2,256,1,16,64]{1,4,3,0,2:T(8,128)(2,1)S(1)} %copy-done.2), kind=kOutput, calls=%fused_computation.26 | convolution fusion | flops 273154048 | bytes 10518528 | tf_op jit(solution)/shard_map/bhqk,bkhd->bqhd/dot_general | solution.py:34
  117.0 0.0 all-gather.5.cloned.1.call-done
  117.0 3.3 %fusion.112 = (f32[2,256]{1,0:T(2,128)S(1)}, f32[2,256,1024]{2,1,0:T(8,128)S(1)}) fusion(bf16[2,256,1024]{1,2,0:T(8,128)(2,1)} %bitcast.134, bf16[1024,1024]{1,0:T(8,128)(2,1)} %all-gather.5.cloned.1.call-done, bf16[2,256,1024]{2,1,0:T(8,128)(2,1)S(1)} %copy-done.1), kind=kOutput, calls=%fused_computation.120 | convolution fusion | flops 1075314176 | bytes 6293504 | tf_op jit(solution)/shard_map/dot_general | solution.py:39
  120.2 0.4 multiply_reduce_fusion.1
  120.6 0.0 copy-done
  120.6 0.5 fusion.54
  121.2 0.2 fusion.113
  121.3 0.5 convolution_convert_fusion.1
  121.8 0.1 copy.37
  122.0 11.3 %all_to_all.10 = bf16[2,32,1024]{2,0,1:T(2,128)(2,1)S(1)} all-to-all(bf16[2,32,1024]{2,0,1:T(2,128)(2,1)S(1)} %copy.37), channel_id=1, replica_groups=mesh['group'=2,'expert'=16] {'expert'}, dimensions={1} | all-to-all | bytes 262144 | tf_op jit(solution)/shard_map/all_to_all | solution.py:55
  133.2 6.1 %fusion.24 = bf16[2,16,1,2,1024]{4,1,3,0,2:T(8,128)(2,1)S(1)} fusion(bf16[1,2048,1024]{2,1,0:T(8,128)(2,1)} %param.11, bf16[1,1024,2048]{2,1,0:T(8,128)(2,1)} %param.10, bf16[2,16,2,1024]{3,0,2,1:T(2,128)(2,1)S(1)} %bitcast.135), kind=kOutput, calls=%fused_computation.29 | convolution fusion | flops 545456128 | bytes 8650752 | tf_op jit(solution)/shard_map/bneph,ehd->bnepd/dot_general | solution.py:62
  139.3 0.8 copy.39
  140.1 3.5 %all-to-all-start.1 = ((bf16[2,32,1024]{2,0,1:T(2,128)(2,1)}), bf16[2,32,1024]{2,0,1:T(2,128)(2,1)S(1)}, u32[]{:S(2)}, u32[]{:S(2)}) async-start(bf16[2,32,1024]{2,0,1:T(2,128)(2,1)} %bitcast.27), calls=%async_computation.1 | async-start | bytes 262144 | tf_op jit(solution)/shard_map/all_to_all | solution.py:66
  143.7 7.9 %all-to-all-done.1 = bf16[2,32,1024]{2,0,1:T(2,128)(2,1)S(1)} async-done(((bf16[2,32,1024]{2,0,1:T(2,128)(2,1)}), bf16[2,32,1024]{2,0,1:T(2,128)(2,1)S(1)}, u32[]{:S(2)}, u32[]{:S(2)}) %all-to-all-start.1) | async-done | bytes 131104 | tf_op jit(solution)/shard_map/all_to_all | solution.py:66
  151.6 1.5 add_convert_fusion
  (5 shorter events, 0.1 us)
Async XLA Ops:
  6.5 114.1 %copy-start = (bf16[1024,32]{0,1:T(8,128)(2,1)S(1)}, bf16[1024,32]{0,1:T(8,128)(2,1)}, u32[]{:S(2)}) copy-start(bf16[1024,32]{0,1:T(8,128)(2,1)} %param.9) | copy-start | bytes 196612
  6.5 2.9 %copy-start.1 = (bf16[2,256,1024]{2,1,0:T(8,128)(2,1)S(1)}, bf16[2,256,1024]{2,1,0:T(8,128)(2,1)}, u32[]{:S(2)}) copy-start(bf16[2,256,1024]{2,1,0:T(8,128)(2,1)} %param.6) | copy-start | bytes 3145732
  6.5 67.7 %all-gather.3.cloned.1.call-start = ((), (), s32[]{:S(2)}) async-start(), calls=%async_computation.2 | async-start | bytes 6684672 | tf_op jit(solution)/shard_map/all_gather | solution.py:24
  7.3 109.7 %all-gather.5.cloned.1.call-start = ((), (), s32[]{:S(2)}) async-start(), calls=%async_computation.3 | async-start | bytes 2228224 | tf_op jit(solution)/shard_map/all_gather | solution.py:38
  108.8 6.3 %copy-start.2 = (bf16[2,256,1,16,64]{1,4,3,0,2:T(8,128)(2,1)S(1)}, bf16[2,256,1,16,64]{1,4,3,0,2:T(8,128)(2,1)}, u32[]{:S(2)}) copy-start(bf16[2,256,1,16,64]{1,4,3,0,2:T(8,128)(2,1)} %copy.47) | copy-start | bytes 3145732
  140.1 11.4 %all-to-all-start.1 = ((bf16[2,32,1024]{2,0,1:T(2,128)(2,1)}), bf16[2,32,1024]{2,0,1:T(2,128)(2,1)S(1)}, u32[]{:S(2)}, u32[]{:S(2)}) async-start(bf16[2,32,1024]{2,0,1:T(2,128)(2,1)} %bitcast.27), calls=%async_computation.1 | async-start | bytes 262144 | tf_op jit(solution)/shard_map/all_to_all | solution.py:66
Sparse Core Ops, SparseCore 0:
  9.6 64.5 all-gather.2
  76.4 39.9 all-gather.4
where the time goes:
time: 160 us
  waiting for transfers between devices  73.3 us (46%)
  local copies, waits for them, and re-layouts  25.1 us (16%)
  matrix products  24 us (15%)
  between operations  13.5 us (8%)
  blocking collectives  11.3 us (7%)
  other arithmetic  9.08 us (6%)
  starting transfers between devices  3.55 us (2%)
    all_gather x1, waiting for transfers between devices, on_device(): full_qkv = lax.all_gather(w_qkv, 'expert', axis=0, tiled=True)  64 us
    all_to_all x1, blocking collectives, on_device(): lax.all_to_all(slot_inputs, 'expert', split_axis=1, concat_axis=1, tiled=...  11.3 us
    unnamed x9, local copies, waits for them, and re-layouts  9.61 us
    reshape x1, local copies, waits for them, and re-layouts, on_device(): qkv.astype(jnp.bfloat16)  8.6 us
    all_to_all x1, waiting for transfers between devices, on_device(): lax.all_to_all(answered, 'expert', split_axis=1, concat_axis=1, tiled=True)  7.85 us
    dot_general x1, matrix products, on_device(): qkv = jnp.dot(normed, full_qkv, preferred_element_type=jnp.float32)  7.53 us
    sub x1, other arithmetic, on_device(): weights = jax.nn.softmax(scores, axis=-1).astype(jnp.bfloat16)  6.31 us
    dot_general x1, matrix products, on_device(): jnp.einsum('bneph,ehd->bnepd', hidden, w_expert_out, preferred_element_ty...  6.09 us
  transfers between devices with their start and end apart: 3, of which 2 were waited for; matrix products, arithmetic and copies ran while one was open for 28% of the time, Pallas kernels for 0%

commit v1 on v0

--- a/solution.py
+++ b/solution.py
@@ -5,6 +5,12 @@
 from jax.sharding import PartitionSpec as P
 
 HEADS = 16
+
+
+def in_order(parts, dim):
+    parts = jnp.moveaxis(parts, 0, dim)
+    shape = parts.shape
+    return parts.reshape(*shape[:dim], shape[dim] * shape[dim + 1], *shape[dim + 2 :])
 
 
 def layer_norm(values):
@@ -21,7 +27,19 @@
     normed = (
         layer_norm(tokens.astype(jnp.float32)).astype(jnp.bfloat16).reshape(row_count, model_width)
     )
-    full_qkv = lax.all_gather(w_qkv, "expert", axis=0, tiled=True)
+    count = lax.axis_size("expert")
+    pairs_2 = [(i, (i + 1) % count) for i in range(count)]
+    back = [(b, a) for a, b in pairs_2]
+    lower, upper = ([], [])
+    for step in range(count - 1):
+        if step % 2 == 0:
+            lower.append(lax.ppermute(lower[-1] if lower else w_qkv, "expert", pairs_2))
+        else:
+            upper.append(lax.ppermute(upper[-1] if upper else w_qkv, "expert", back))
+    blocks = jnp.stack([*lower[::-1], w_qkv, *upper])
+    shift = lax.axis_index("expert") - len(lower)
+    blocks = blocks[(jnp.arange(count) - shift) % count]
+    full_qkv = in_order(blocks, 0)
     qkv = jnp.dot(normed, full_qkv, preferred_element_type=jnp.float32)
     packed = qkv.astype(jnp.bfloat16).reshape(image_count, length, 3, head_count, head_width)
     query = packed[:, :, 0]

time: 160 us -> 201 us (1.26)
  starting transfers between devices: 3.55 us -> 36.2 us
  waiting for transfers between devices: 73.3 us -> 53 us
  local copies, waits for them, and re-layouts: 25.1 us -> 43.2 us
  blocking collectives: 11.3 us -> 18.8 us
  other arithmetic: 9.08 us -> 12.6 us
    all_gather x1 -> x0, waiting for transfers between devices: 64 us -> none  [on_device(): full_qkv = lax.all_gather(w_qkv, 'expert', axis=0, tiled=True)]
    ppermute x0 -> x15, waiting for transfers between devices: none -> 45.1 us  [the longest x8 45.1 us: on_device(): lower.append(lax.ppermute(lower[-1] if lower else w_qkv, 'expert', pairs_2))]
    ppermute x0 -> x15, starting transfers between devices: none -> 32.7 us  [the longest x7 28.1 us: on_device(): upper.append(lax.ppermute(upper[-1] if upper else w_qkv, 'expert', back))]
    unnamed x9 -> x30, local copies, waits for them, and re-layouts: 9.61 us -> 22.9 us
    all_to_all x1, blocking collectives: 11.3 us -> 18.8 us  [on_device(): lax.all_to_all(slot_inputs, 'expert', split_axis=1, concat_axis=1, tiled=...]
    gather x0 -> x1, local copies, waits for them, and re-layouts: none -> 6.39 us  [on_device(): blocks = blocks[(jnp.arange(count) - shift) % count]]
    reshape x1, local copies, waits for them, and re-layouts: 8.6 us -> 6.12 us  [on_device(): qkv.astype(jnp.bfloat16)]
    convert_element_type x1, other arithmetic: 0.32 us -> 2.5 us  [on_device(): layer_norm(tokens.astype(jnp.float32)).astype(jnp.bfloat16)]
  transfers between devices with their start and end apart: 3 -> 17, of which waited for: 2 -> 9; matrix products, arithmetic and copies ran while one was open for 28% -> 32% of each run, Pallas kernels for 0% -> 0%
where the time goes in v1:
time: 201 us; the launch traced here: 200 us
  waiting for transfers between devices  53 us (26%)
  local copies, waits for them, and re-layouts  43.2 us (21%)
  starting transfers between devices  36.2 us (18%)
  matrix products  22.7 us (11%)
  blocking collectives  18.8 us (9%)
  between operations  13.5 us (7%)
  other arithmetic  12.6 us (6%)
    ppermute x8, waiting for transfers between devices, on_device(): lower.append(lax.ppermute(lower[-1] if lower else w_qkv, 'expert', pairs_2))  45.1 us
    ppermute x7, starting transfers between devices, on_device(): upper.append(lax.ppermute(upper[-1] if upper else w_qkv, 'expert', back))  28.1 us
    unnamed x30, local copies, waits for them, and re-layouts  22.9 us
    all_to_all x1, blocking collectives, on_device(): lax.all_to_all(slot_inputs, 'expert', split_axis=1, concat_axis=1, tiled=...  18.8 us
    all_to_all x1, waiting for transfers between devices, on_device(): lax.all_to_all(answered, 'expert', split_axis=1, concat_axis=1, tiled=True)  7.85 us
    dot_general x1, matrix products, on_device(): qkv = jnp.dot(normed, full_qkv, preferred_element_type=jnp.float32)  6.54 us
    gather x1, local copies, waits for them, and re-layouts, on_device(): blocks = blocks[(jnp.arange(count) - shift) % count]  6.39 us
    sub x1, other arithmetic, on_device(): weights = jax.nn.softmax(scores, axis=-1).astype(jnp.bfloat16)  6.31 us
  transfers between devices with their start and end apart: 17, of which 9 were waited for; matrix products, arithmetic and copies ran while one was open for 32% of the time, Pallas kernels for 0%

profile of v1, /device:TPU:0, one launch (start us, length us, event | category | flops | bytes accessed | tf_op | source)
XLA Modules:
  0.0 200.1 jit_solution(4644941336463404335)
XLA Ops:
  7.0 10.7 %collective-permute-done = bf16[64,3072]{1,0:T(8,128)(2,1)S(1)} collective-permute-done((bf16[64,3072]{1,0:T(8,128)(2,1)}, bf16[64,3072]{1,0:T(8,128)(2,1)S(1)}, u32[]{:S(2)}, u32[]{:S(2)}) %collective-permute-start) | collective-permute-done | bytes 393248 | tf_op jit(solution)/shard_map/ppermute | solution.py:36
  17.7 4.4 %collective-permute-start.8 = (bf16[64,3072]{1,0:T(8,128)(2,1)}, bf16[64,3072]{1,0:T(8,128)(2,1)S(1)}, u32[]{:S(2)}, u32[]{:S(2)}) collective-permute-start(bf16[64,3072]{1,0:T(8,128)(2,1)} %param.7), channel_id=1, source_target_pairs={{1,0},{2,1},{3,2},{4,3},{5,4},{6,5},{7,6},{8,7},{9,8},{10,9},{11,1... | collective-permute-start | bytes 1179656 | tf_op jit(solution)/shard_map/ppermute | solution.py:38
  22.1 5.6 %collective-permute-done.1 = bf16[64,3072]{1,0:T(8,128)(2,1)S(1)} collective-permute-done((bf16[64,3072]{1,0:T(8,128)(2,1)S(1)}, bf16[64,3072]{1,0:T(8,128)(2,1)S(1)}, u32[]{:S(2)}, u32[]{:S(2)}) %collective-permute-start.1) | collective-permute-done | bytes 393248 | tf_op jit(solution)/shard_map/ppermute | solution.py:36
  27.7 4.6 %collective-permute-start.9 = (bf16[64,3072]{1,0:T(8,128)(2,1)S(1)}, bf16[64,3072]{1,0:T(8,128)(2,1)S(1)}, u32[]{:S(2)}, u32[]{:S(2)}) collective-permute-start(bf16[64,3072]{1,0:T(8,128)(2,1)S(1)} %collective-permute-done.8), channel_id=1, source_target_pairs={{1,0},{2,1},{3,2},{4,3},{5,4},{6,5},{7,6},{8,7},{9,8},{10,9},{11,1... | collective-permute-start | bytes 1179656 | tf_op jit(solution)/shard_map/ppermute | solution.py:38
  32.3 5.4 %collective-permute-done.2 = bf16[64,3072]{1,0:T(8,128)(2,1)S(1)} collective-permute-done((bf16[64,3072]{1,0:T(8,128)(2,1)S(1)}, bf16[64,3072]{1,0:T(8,128)(2,1)S(1)}, u32[]{:S(2)}, u32[]{:S(2)}) %collective-permute-start.2) | collective-permute-done | bytes 393248 | tf_op jit(solution)/shard_map/ppermute | solution.py:36
  37.7 4.6 %collective-permute-start.10 = (bf16[64,3072]{1,0:T(8,128)(2,1)S(1)}, bf16[64,3072]{1,0:T(8,128)(2,1)S(1)}, u32[]{:S(2)}, u32[]{:S(2)}) collective-permute-start(bf16[64,3072]{1,0:T(8,128)(2,1)S(1)} %collective-permute-done.9), channel_id=1, source_target_pairs={{1,0},{2,1},{3,2},{4,3},{5,4},{6,5},{7,6},{8,7},{9,8},{10,9},{11,1... | collective-permute-start | bytes 1179656 | tf_op jit(solution)/shard_map/ppermute | solution.py:38
  42.3 5.4 %collective-permute-done.3 = bf16[64,3072]{1,0:T(8,128)(2,1)S(1)} collective-permute-done((bf16[64,3072]{1,0:T(8,128)(2,1)S(1)}, bf16[64,3072]{1,0:T(8,128)(2,1)S(1)}, u32[]{:S(2)}, u32[]{:S(2)}) %collective-permute-start.3) | collective-permute-done | bytes 393248 | tf_op jit(solution)/shard_map/ppermute | solution.py:36
  48.5 3.9 %collective-permute-start.11 = (bf16[64,3072]{1,0:T(8,128)(2,1)S(1)}, bf16[64,3072]{1,0:T(8,128)(2,1)S(1)}, u32[]{:S(2)}, u32[]{:S(2)}) collective-permute-start(bf16[64,3072]{1,0:T(8,128)(2,1)S(1)} %collective-permute-done.10), channel_id=1, source_target_pairs={{1,0},{2,1},{3,2},{4,3},{5,4},{6,5},{7,6},{8,7},{9,8},{10,9},{11,1... | collective-permute-start | bytes 1179656 | tf_op jit(solution)/shard_map/ppermute | solution.py:38
  52.4 5.5 %collective-permute-done.4 = bf16[64,3072]{1,0:T(8,128)(2,1)} collective-permute-done((bf16[64,3072]{1,0:T(8,128)(2,1)S(1)}, bf16[64,3072]{1,0:T(8,128)(2,1)}, u32[]{:S(2)}, u32[]{:S(2)}) %collective-permute-start.4) | collective-permute-done | bytes 393248 | tf_op jit(solution)/shard_map/ppermute | solution.py:36
  57.8 0.9 collective-permute-start.5
  58.7 1.5 convert_reduce_fusion
  60.2 3.6 %collective-permute-start.12 = (bf16[64,3072]{1,0:T(8,128)(2,1)S(1)}, bf16[64,3072]{1,0:T(8,128)(2,1)S(1)}, u32[]{:S(2)}, u32[]{:S(2)}) collective-permute-start(bf16[64,3072]{1,0:T(8,128)(2,1)S(1)} %collective-permute-done.11), channel_id=1, source_target_pairs={{1,0},{2,1},{3,2},{4,3},{5,4},{6,5},{7,6},{8,7},{9,8},{10,9},{11,1... | collective-permute-start | bytes 1179656 | tf_op jit(solution)/shard_map/ppermute | solution.py:38
  63.9 4.3 %collective-permute-done.5 = bf16[64,3072]{1,0:T(8,128)(2,1)} collective-permute-done((bf16[64,3072]{1,0:T(8,128)(2,1)}, bf16[64,3072]{1,0:T(8,128)(2,1)}, u32[]{:S(2)}, u32[]{:S(2)}) %collective-permute-start.5) | collective-permute-done | bytes 393248 | tf_op jit(solution)/shard_map/ppermute | solution.py:36
  68.1 2.5 %collective-permute-start.6 = (bf16[64,3072]{1,0:T(8,128)(2,1)}, bf16[64,3072]{1,0:T(8,128)(2,1)S(1)}, u32[]{:S(2)}, u32[]{:S(2)}) collective-permute-start(bf16[64,3072]{1,0:T(8,128)(2,1)} %collective-permute-done.5), channel_id=1, source_target_pairs={{0,1},{1,2},{2,3},{3,4},{4,5},{5,6},{6,7},{7,8},{8,9},{9,10},{10,1... | collective-permute-start | bytes 1179656 | tf_op jit(solution)/shard_map/ppermute | solution.py:36
  70.6 1.6 fusion.14
  72.3 3.0 %collective-permute-start.13 = (bf16[64,3072]{1,0:T(8,128)(2,1)S(1)}, bf16[64,3072]{1,0:T(8,128)(2,1)S(1)}, u32[]{:S(2)}, u32[]{:S(2)}) collective-permute-start(bf16[64,3072]{1,0:T(8,128)(2,1)S(1)} %collective-permute-done.12), channel_id=1, source_target_pairs={{1,0},{2,1},{3,2},{4,3},{5,4},{6,5},{7,6},{8,7},{9,8},{10,9},{11,1... | collective-permute-start | bytes 1179656 | tf_op jit(solution)/shard_map/ppermute | solution.py:38
  75.2 5.3 %collective-permute-done.6 = bf16[64,3072]{1,0:T(8,128)(2,1)S(1)} collective-permute-done((bf16[64,3072]{1,0:T(8,128)(2,1)}, bf16[64,3072]{1,0:T(8,128)(2,1)S(1)}, u32[]{:S(2)}, u32[]{:S(2)}) %collective-permute-start.6) | collective-permute-done | bytes 393248 | tf_op jit(solution)/shard_map/ppermute | solution.py:36
  81.0 2.5 %fusion.15 = bf16[2,256,1024]{2,1,0:T(8,128)(2,1)} fusion(bf16[2,256,1024]{2,1,0:T(8,128)(2,1)} %param.6, f32[2,256]{1,0:T(2,128)S(1)} %add_rsqrt_fusion.1, f32[2,256]{1,0:T(2,128)S(1)} %broadcast_multiply_fusion.1), kind=kLoop, calls=%fused_computation.21 | loop fusion | flops 2097152 | bytes 2101248 | tf_op jit(solution)/shard_map/convert_element_type | solution.py:28
  83.5 4.0 %collective-permute-start.14 = (bf16[64,3072]{1,0:T(8,128)(2,1)S(1)}, bf16[64,3072]{1,0:T(8,128)(2,1)S(1)}, u32[]{:S(2)}, u32[]{:S(2)}) collective-permute-start(bf16[64,3072]{1,0:T(8,128)(2,1)S(1)} %collective-permute-done.13), channel_id=1, source_target_pairs={{1,0},{2,1},{3,2},{4,3},{5,4},{6,5},{7,6},{8,7},{9,8},{10,9},{11,1... | collective-permute-start | bytes 1179656 | tf_op jit(solution)/shard_map/ppermute | solution.py:38
  87.5 3.0 %collective-permute-done.7 = bf16[64,3072]{1,0:T(8,128)(2,1)S(1)} collective-permute-done((bf16[64,3072]{1,0:T(8,128)(2,1)S(1)}, bf16[64,3072]{1,0:T(8,128)(2,1)S(1)}, u32[]{:S(2)}, u32[]{:S(2)}) %collective-permute-start.7) | collective-permute-done | bytes 393248 | tf_op jit(solution)/shard_map/ppermute | solution.py:36
  91.3 0.8 bitcast_dynamic-update-slice_fusion.14
  92.1 1.8 bitcast_dynamic-update-slice_fusion.13
  93.9 1.8 bitcast_dynamic-update-slice_fusion.12
  96.4 0.8 bitcast_dynamic-update-slice_fusion.10
  97.2 0.8 bitcast_dynamic-update-slice_fusion.9
  98.0 0.8 bitcast_dynamic-update-slice_fusion.8
  101.1 0.8 bitcast_dynamic-update-slice_fusion.4
  101.9 0.8 bitcast_dynamic-update-slice_fusion.3
  102.6 0.8 bitcast_dynamic-update-slice_fusion.2
  103.4 0.8 bitcast_dynamic-update-slice_fusion.1
  104.2 0.8 bitcast_dynamic-update-slice_fusion
  105.0 6.4 %gather_fusion = bf16[16,64,3072]{2,1,0:T(8,128)(2,1)} fusion(bf16[16,64,3072]{2,1,0:T(8,128)(2,1)} %bitcast_dynamic-update-slice_fusion, s32[1024]{0:T(1024)S(1)} %pad_clamp_fusion), kind=kCustom, calls=%fused_computation | custom fusion | bytes 12582976 | tf_op jit(solution)/shard_map/gather | solution.py:41
  111.4 6.5 %convolution_convert_fusion = bf16[512,3072]{1,0:T(8,128)(2,1)S(1)} fusion(bf16[512,1024]{1,0:T(8,128)(2,1)} %bitcast.169, bf16[1024,3072]{1,0:T(8,128)(2,1)} %bitcast.168), kind=kOutput, calls=%fused_computation.8 | convolution fusion | flops 3222798336 | bytes 10485760 | tf_op jit(solution)/shard_map/dot_general | solution.py:43
  117.9 6.1 %reshape.141 = bf16[2,256,3,16,64]{4,3,2,1,0:T(8,128)(2,1)} reshape(bf16[512,3072]{1,0:T(8,128)(2,1)S(1)} %convolution_convert_fusion) | data formatting | bytes 6291456 | tf_op jit(solution)/shard_map/reshape | solution.py:44
  124.1 6.0 %fusion.112 = (bf16[2,256,1,16,64]{4,3,2,1,0:T(8,128)(2,1)S(1)}, bf16[2,256,1,16,64]{4,3,2,1,0:T(8,128)(2,1)}, bf16[2,256,1,16,64]{4,3,2,1,0:T(8,128)(2,1)}) fusion(bf16[2,256,3,16,64]{4,3,2,1,0:T(8,128)(2,1)} %reshape.141), kind=kLoop, calls=%fused_computation.142 | loop fusion | bytes 6291456 | tf_op jit(solution)/shard_map/slice | solution.py:47
  130.1 2.8 %copy.48 = bf16[2,256,1,16,64]{1,4,3,0,2:T(8,128)(2,1)S(1)} copy(bf16[2,256,1,16,64]{4,3,2,1,0:T(8,128)(2,1)} %get-tuple-element.6) | data formatting | bytes 2097152
  132.9 3.6 %copy.49 = bf16[2,256,1,16,64]{1,4,3,0,2:T(8,128)(2,1)} copy(bf16[2,256,1,16,64]{4,3,2,1,0:T(8,128)(2,1)} %get-tuple-element.7) | data formatting | bytes 2097152
  136.4 2.5 %copy.47 = bf16[2,256,1,16,64]{1,4,3,0,2:T(8,128)(2,1)} copy(bf16[2,256,1,16,64]{4,3,2,1,0:T(8,128)(2,1)S(1)} %get-tuple-element.5) | data formatting | bytes 2097152
  138.9 2.5 %fusion.31 = f32[2,16,256,256]{2,3,1,0:T(8,128)S(1)} fusion(bf16[2,256,1,16,64]{1,4,3,0,2:T(8,128)(2,1)} %copy.49, bf16[2,256,1,16,64]{1,4,3,0,2:T(8,128)(2,1)S(1)} %copy.48), kind=kOutput, calls=%fused_computation.35 | convolution fusion | flops 268435456 | bytes 10485760 | tf_op jit(solution)/shard_map/bqhd,bkhd->bhqk/dot_general | solution.py:48
  141.5 6.3 %fusion.113 = (f32[2,16,256]{2,1,0:T(8,128)S(1)}, f32[2,16,256,256]{2,3,1,0:T(8,128)S(1)}) fusion(f32[2,16,256,256]{2,3,1,0:T(8,128)S(1)} %fusion.31), kind=kOutput, calls=%fused_computation.143 | output fusion | flops 8388863 | bytes 16809984 | tf_op jit(solution)/shard_map/sub | solution.py:51
  147.8 1.8 fusion.20
  149.6 3.3 %fusion.114 = (f32[2,256]{1,0:T(2,128)S(1)}, f32[2,256,1024]{2,1,0:T(8,128)S(1)}) fusion(bf16[2,256,1024]{1,2,0:T(8,128)(2,1)} %bitcast.170, bf16[1024,1024]{1,0:T(8,128)(2,1)} %all-gather.2.cloned.1.call-done, bf16[2,256,1024]{2,1,0:T(8,128)(2,1)S(1)} %copy-done.1), kind=kOutput, calls=%fused_computation.144 | convolution fusion | flops 1075314176 | bytes 6293504 | tf_op jit(solution)/shard_map/dot_general | solution.py:57
  154.6 18.8 %all_to_all.10 = bf16[2,32,1024]{2,0,1:T(2,128)(2,1)S(1)} all-to-all(bf16[2,32,1024]{2,0,1:T(2,128)(2,1)S(1)} %copy.37), channel_id=1, replica_groups=mesh['group'=2,'expert'=16] {'expert'}, dimensions={1} | all-to-all | bytes 262144 | tf_op jit(solution)/shard_map/all_to_all | solution.py:73
  173.5 6.1 %fusion.24 = bf16[2,16,1,2,1024]{4,1,3,0,2:T(8,128)(2,1)S(1)} fusion(bf16[1,2048,1024]{2,1,0:T(8,128)(2,1)} %param.11, bf16[1,1024,2048]{2,1,0:T(8,128)(2,1)} %param.10, bf16[2,16,2,1024]{3,0,2,1:T(2,128)(2,1)S(1)} %bitcast.171), kind=kOutput, calls=%fused_computation.30 | convolution fusion | flops 545456128 | bytes 8650752 | tf_op jit(solution)/shard_map/bneph,ehd->bnepd/dot_general | solution.py:80
  179.6 0.8 copy.39
  180.3 3.5 %all-to-all-start.1 = ((bf16[2,32,1024]{2,0,1:T(2,128)(2,1)}), bf16[2,32,1024]{2,0,1:T(2,128)(2,1)S(1)}, u32[]{:S(2)}, u32[]{:S(2)}) async-start(bf16[2,32,1024]{2,0,1:T(2,128)(2,1)} %bitcast.45), calls=%async_computation.1 | async-start | bytes 262144 | tf_op jit(solution)/shard_map/all_to_all | solution.py:84
  183.9 7.9 %all-to-all-done.1 = bf16[2,32,1024]{2,0,1:T(2,128)(2,1)S(1)} async-done(((bf16[2,32,1024]{2,0,1:T(2,128)(2,1)}), bf16[2,32,1024]{2,0,1:T(2,128)(2,1)S(1)}, u32[]{:S(2)}, u32[]{:S(2)}) %all-to-all-start.1) | async-done | bytes 131104 | tf_op jit(solution)/shard_map/all_to_all | solution.py:84
  191.8 1.5 add_convert_fusion
  (45 shorter events, 7.4 us)
Async XLA Ops:
  6.5 146.7 %copy-start = (bf16[1024,32]{0,1:T(8,128)(2,1)S(1)}, bf16[1024,32]{0,1:T(8,128)(2,1)}, u32[]{:S(2)}) copy-start(bf16[1024,32]{0,1:T(8,128)(2,1)} %param.9) | copy-start | bytes 196612
  6.5 92.2 %copy-start.3 = (bf16[64,3072]{1,0:T(8,128)(2,1)S(1)}, bf16[64,3072]{1,0:T(8,128)(2,1)}, u32[]{:S(2)}) copy-start(bf16[64,3072]{1,0:T(8,128)(2,1)} %param.7) | copy-start | bytes 1179652
  6.5 143.1 %all-gather.2.cloned.1.call-start = ((), (), s32[]{:S(2)}) async-start(), calls=%async_computation.2 | async-start | bytes 2228224 | tf_op jit(solution)/shard_map/all_gather | solution.py:56
  6.5 11.1 %collective-permute-start = (bf16[64,3072]{1,0:T(8,128)(2,1)}, bf16[64,3072]{1,0:T(8,128)(2,1)S(1)}, u32[]{:S(2)}, u32[]{:S(2)}) collective-permute-start(bf16[64,3072]{1,0:T(8,128)(2,1)} %param.7), channel_id=1, source_target_pairs={{0,1},{1,2},{2,3},{3,4},{4,5},{5,6},{6,7},{7,8},{8,9},{9,10},{10,1... | collective-permute-start | bytes 1179656 | tf_op jit(solution)/shard_map/ppermute | solution.py:36
  17.7 10.0 %collective-permute-start.1 = (bf16[64,3072]{1,0:T(8,128)(2,1)S(1)}, bf16[64,3072]{1,0:T(8,128)(2,1)S(1)}, u32[]{:S(2)}, u32[]{:S(2)}) collective-permute-start(bf16[64,3072]{1,0:T(8,128)(2,1)S(1)} %collective-permute-done), channel_id=1, source_target_pairs={{0,1},{1,2},{2,3},{3,4},{4,5},{5,6},{6,7},{7,8},{8,9},{9,10},{10,1... | collective-permute-start | bytes 1179656 | tf_op jit(solution)/shard_map/ppermute | solution.py:36
  17.7 10.1 %collective-permute-start.8 = (bf16[64,3072]{1,0:T(8,128)(2,1)}, bf16[64,3072]{1,0:T(8,128)(2,1)S(1)}, u32[]{:S(2)}, u32[]{:S(2)}) collective-permute-start(bf16[64,3072]{1,0:T(8,128)(2,1)} %param.7), channel_id=1, source_target_pairs={{1,0},{2,1},{3,2},{4,3},{5,4},{6,5},{7,6},{8,7},{9,8},{10,9},{11,1... | collective-permute-start | bytes 1179656 | tf_op jit(solution)/shard_map/ppermute | solution.py:38
  27.7 10.0 %collective-permute-start.2 = (bf16[64,3072]{1,0:T(8,128)(2,1)S(1)}, bf16[64,3072]{1,0:T(8,128)(2,1)S(1)}, u32[]{:S(2)}, u32[]{:S(2)}) collective-permute-start(bf16[64,3072]{1,0:T(8,128)(2,1)S(1)} %collective-permute-done.1), channel_id=1, source_target_pairs={{0,1},{1,2},{2,3},{3,4},{4,5},{5,6},{6,7},{7,8},{8,9},{9,10},{10,1... | collective-permute-start | bytes 1179656 | tf_op jit(solution)/shard_map/ppermute | solution.py:36
  27.7 10.0 %collective-permute-start.9 = (bf16[64,3072]{1,0:T(8,128)(2,1)S(1)}, bf16[64,3072]{1,0:T(8,128)(2,1)S(1)}, u32[]{:S(2)}, u32[]{:S(2)}) collective-permute-start(bf16[64,3072]{1,0:T(8,128)(2,1)S(1)} %collective-permute-done.8), channel_id=1, source_target_pairs={{1,0},{2,1},{3,2},{4,3},{5,4},{6,5},{7,6},{8,7},{9,8},{10,9},{11,1... | collective-permute-start | bytes 1179656 | tf_op jit(solution)/shard_map/ppermute | solution.py:38
  37.7 10.0 %collective-permute-start.3 = (bf16[64,3072]{1,0:T(8,128)(2,1)S(1)}, bf16[64,3072]{1,0:T(8,128)(2,1)S(1)}, u32[]{:S(2)}, u32[]{:S(2)}) collective-permute-start(bf16[64,3072]{1,0:T(8,128)(2,1)S(1)} %collective-permute-done.2), channel_id=1, source_target_pairs={{0,1},{1,2},{2,3},{3,4},{4,5},{5,6},{6,7},{7,8},{8,9},{9,10},{10,1... | collective-permute-start | bytes 1179656 | tf_op jit(solution)/shard_map/ppermute | solution.py:36
  37.7 10.3 %collective-permute-start.10 = (bf16[64,3072]{1,0:T(8,128)(2,1)S(1)}, bf16[64,3072]{1,0:T(8,128)(2,1)S(1)}, u32[]{:S(2)}, u32[]{:S(2)}) collective-permute-start(bf16[64,3072]{1,0:T(8,128)(2,1)S(1)} %collective-permute-done.9), channel_id=1, source_target_pairs={{1,0},{2,1},{3,2},{4,3},{5,4},{6,5},{7,6},{8,7},{9,8},{10,9},{11,1... | collective-permute-start | bytes 1179656 | tf_op jit(solution)/shard_map/ppermute | solution.py:38
  47.7 0.8 copy-start.4
  47.7 10.1 %collective-permute-start.4 = (bf16[64,3072]{1,0:T(8,128)(2,1)S(1)}, bf16[64,3072]{1,0:T(8,128)(2,1)}, u32[]{:S(2)}, u32[]{:S(2)}) collective-permute-start(bf16[64,3072]{1,0:T(8,128)(2,1)S(1)} %collective-permute-done.3), channel_id=1, source_target_pairs={{0,1},{1,2},{2,3},{3,4},{4,5},{5,6},{6,7},{7,8},{8,9},{9,10},{10,1... | collective-permute-start | bytes 1179656 | tf_op jit(solution)/shard_map/ppermute | solution.py:36
  48.5 11.7 %collective-permute-start.11 = (bf16[64,3072]{1,0:T(8,128)(2,1)S(1)}, bf16[64,3072]{1,0:T(8,128)(2,1)S(1)}, u32[]{:S(2)}, u32[]{:S(2)}) collective-permute-start(bf16[64,3072]{1,0:T(8,128)(2,1)S(1)} %collective-permute-done.10), channel_id=1, source_target_pairs={{1,0},{2,1},{3,2},{4,3},{5,4},{6,5},{7,6},{8,7},{9,8},{10,9},{11,1... | collective-permute-start | bytes 1179656 | tf_op jit(solution)/shard_map/ppermute | solution.py:38
  57.8 10.3 %collective-permute-start.5 = (bf16[64,3072]{1,0:T(8,128)(2,1)}, bf16[64,3072]{1,0:T(8,128)(2,1)}, u32[]{:S(2)}, u32[]{:S(2)}) collective-permute-start(bf16[64,3072]{1,0:T(8,128)(2,1)} %collective-permute-done.4), channel_id=1, source_target_pairs={{0,1},{1,2},{2,3},{3,4},{4,5},{5,6},{6,7},{7,8},{8,9},{9,10},{10,1... | collective-permute-start | bytes 1179656 | tf_op jit(solution)/shard_map/ppermute | solution.py:36
  58.7 37.0 %copy-start.5 = (bf16[64,3072]{1,0:T(8,128)(2,1)S(1)}, bf16[64,3072]{1,0:T(8,128)(2,1)}, u32[]{:S(2)}) copy-start(bf16[64,3072]{1,0:T(8,128)(2,1)} %copy-done.4) | copy-start | bytes 1179652
  60.2 12.0 %collective-permute-start.12 = (bf16[64,3072]{1,0:T(8,128)(2,1)S(1)}, bf16[64,3072]{1,0:T(8,128)(2,1)S(1)}, u32[]{:S(2)}, u32[]{:S(2)}) collective-permute-start(bf16[64,3072]{1,0:T(8,128)(2,1)S(1)} %collective-permute-done.11), channel_id=1, source_target_pairs={{1,0},{2,1},{3,2},{4,3},{5,4},{6,5},{7,6},{8,7},{9,8},{10,9},{11,1... | collective-permute-start | bytes 1179656 | tf_op jit(solution)/shard_map/ppermute | solution.py:38
  68.1 12.4 %collective-permute-start.6 = (bf16[64,3072]{1,0:T(8,128)(2,1)}, bf16[64,3072]{1,0:T(8,128)(2,1)S(1)}, u32[]{:S(2)}, u32[]{:S(2)}) collective-permute-start(bf16[64,3072]{1,0:T(8,128)(2,1)} %collective-permute-done.5), channel_id=1, source_target_pairs={{0,1},{1,2},{2,3},{3,4},{4,5},{5,6},{6,7},{7,8},{8,9},{9,10},{10,1... | collective-permute-start | bytes 1179656 | tf_op jit(solution)/shard_map/ppermute | solution.py:36
  72.3 11.3 %collective-permute-start.13 = (bf16[64,3072]{1,0:T(8,128)(2,1)S(1)}, bf16[64,3072]{1,0:T(8,128)(2,1)S(1)}, u32[]{:S(2)}, u32[]{:S(2)}) collective-permute-start(bf16[64,3072]{1,0:T(8,128)(2,1)S(1)} %collective-permute-done.12), channel_id=1, source_target_pairs={{1,0},{2,1},{3,2},{4,3},{5,4},{6,5},{7,6},{8,7},{9,8},{10,9},{11,1... | collective-permute-start | bytes 1179656 | tf_op jit(solution)/shard_map/ppermute | solution.py:38
  80.5 10.0 %collective-permute-start.7 = (bf16[64,3072]{1,0:T(8,128)(2,1)S(1)}, bf16[64,3072]{1,0:T(8,128)(2,1)S(1)}, u32[]{:S(2)}, u32[]{:S(2)}) collective-permute-start(bf16[64,3072]{1,0:T(8,128)(2,1)S(1)} %collective-permute-done.6), channel_id=1, source_target_pairs={{0,1},{1,2},{2,3},{3,4},{4,5},{5,6},{6,7},{7,8},{8,9},{9,10},{10,1... | collective-permute-start | bytes 1179656 | tf_op jit(solution)/shard_map/ppermute | solution.py:36
  83.5 20.7 %collective-permute-start.14 = (bf16[64,3072]{1,0:T(8,128)(2,1)S(1)}, bf16[64,3072]{1,0:T(8,128)(2,1)S(1)}, u32[]{:S(2)}, u32[]{:S(2)}) collective-permute-start(bf16[64,3072]{1,0:T(8,128)(2,1)S(1)} %collective-permute-done.13), channel_id=1, source_target_pairs={{1,0},{2,1},{3,2},{4,3},{5,4},{6,5},{7,6},{8,7},{9,8},{10,9},{11,1... | collective-permute-start | bytes 1179656 | tf_op jit(solution)/shard_map/ppermute | solution.py:38
  141.5 6.3 %copy-start.2 = (bf16[2,256,1,16,64]{1,4,3,0,2:T(8,128)(2,1)S(1)}, bf16[2,256,1,16,64]{1,4,3,0,2:T(8,128)(2,1)}, u32[]{:S(2)}) copy-start(bf16[2,256,1,16,64]{1,4,3,0,2:T(8,128)(2,1)} %copy.47) | copy-start | bytes 3145732
  147.8 1.8 copy-start.1
  180.3 11.4 %all-to-all-start.1 = ((bf16[2,32,1024]{2,0,1:T(2,128)(2,1)}), bf16[2,32,1024]{2,0,1:T(2,128)(2,1)S(1)}, u32[]{:S(2)}, u32[]{:S(2)}) async-start(bf16[2,32,1024]{2,0,1:T(2,128)(2,1)} %bitcast.45), calls=%async_computation.1 | async-start | bytes 262144 | tf_op jit(solution)/shard_map/all_to_all | solution.py:84
Sparse Core Ops, SparseCore 0:
  58.8 46.6 all-gather.1
